TPU v7x, 32 devices: a whole 2x2x4 slice. The times are simulated.
32 devices in a mesh: seq: 8 (over z, y), tp: 4 (over x, core).
Axes of the slice: x: 2, y: 2, z: 4, core: 2. Of those that a mesh axis runs over, the one named last changes fastest.
Arguments:
- layer_activation: bfloat16 [3072, 2048], P('seq', 'tp'), may hold values from -6 to 6
- sequence_label: int32 [3072], P('seq'), may hold values from 0 to 2, as said below
- sequence_extents: int32 [2], replicated, may hold values from 1 to 1920, as said below
- destination_slots: int32 [2], replicated, may hold values from 0 to 7, as said below
- entry_layernorm_coef: float32 [2048], replicated, may hold values from 0.5 to 1.5
- lagged_blend_coefs: float32 [6, 2048], replicated, may hold values from 0 to 1
- query_matrix: bfloat16 [2048, 2048], P(None, 'tp'), may hold values from -0.125 to 0.125
- lookup_matrix: bfloat16 [2048, 2048], P(None, 'tp'), may hold values from -0.125 to 0.125
- content_matrix: bfloat16 [2048, 2048], P(None, 'tp'), may hold values from -0.125 to 0.125
- readout_matrix: bfloat16 [2048, 2048], P('tp'), may hold values from -0.125 to 0.125
- forgetting_narrow_matrix: bfloat16 [2048, 96], replicated, may hold values from -0.125 to 0.125
- forgetting_widen_matrix: bfloat16 [96, 2048], P(None, 'tp'), may hold values from -2.5 to 2.5
- forgetting_offset: float32 [2048], P('tp'), may hold values from -11 to -3.5
- stepsize_narrow_matrix: bfloat16 [2048, 96], replicated, may hold values from -0.125 to 0.125
- stepsize_widen_matrix: bfloat16 [96, 2048], P(None, 'tp'), may hold values from -0.625 to 0.625
- stepsize_offset: float32 [2048], P('tp'), may hold values from -4 to 4
- gating_narrow_matrix: bfloat16 [2048, 256], replicated, may hold values from -0.125 to 0.125
- gating_widen_matrix: bfloat16 [256, 2048], P(None, 'tp'), may hold values from -0.375 to 0.375
- erasure_lookup_coef: float32 [2048], P('tp'), may hold values from 0.5 to 1.5
- lookup_step_fraction: float32 [2048], P('tp'), may hold values from 0 to 1
- diagonal_reward_coef: float32 [2048], P('tp'), may hold values from -3 to 3
- group_layernorm_coef: float32 [2048], P('tp'), may hold values from 0.5 to 1.5
Outputs:
- mixed: bfloat16 [3072, 2048], P('seq', 'tp')
- final_states: float32 [8, 32, 64, 64], P('seq', 'tp')
- final_rows: bfloat16 [8, 2048], P('seq', 'tp')
Inputs may be any that keep to these rules, and one draw needn't show every extreme that they name: `sequence_label`: token p is in prompt 0 for p < sequence_extents[0], in prompt 1 for the next sequence_extents[1] tokens, and padding (2) after them; at least one padding token. `sequence_extents`: one length is exactly 1920, the other at least 768; their sum is under 3072. `destination_slots`: the two owners differ, and one of them is the last index of seq.
All inputs are finite; a program needn't handle non-finite values.
Results may differ from a plain program's by a relative error of at most 0.012.
Values may be sent and summed in bfloat16 or wider, within the bound.
A program may use at most 128 MiB of HBM per device.

v0:
```python
import jax
import jax.numpy as jnp
from jax import lax
from jax.sharding import PartitionSpec as P

CHANNELS_PER_ONE = 64
PROMPTS = 2
EPS = 1e-05
GROUP_EPS = 0.00064


def from_behind(array, axis, by):
    length = lax.axis_size(axis)
    pairs = [(i, i + by) for i in range(length) if 0 <= i + by < length]
    return lax.ppermute(array, axis, pairs)


def broadcast(value, axis, source):
    kept = jnp.where(lax.axis_index(axis) == source, value, 0).astype(value.dtype)
    return lax.psum(kept, axis)


def matmul(left, right):
    return jnp.dot(left, right, preferred_element_type=jnp.float32)


def compose(earlier_map, later_map):
    return jnp.einsum("hij,hjk->hik", earlier_map, later_map, precision=lax.Precision.HIGHEST)


def on_device(
    layer_activation,
    sequence_label,
    sequence_extents,
    destination_slots,
    entry_layernorm_coef,
    lagged_blend_coefs,
    query_matrix,
    lookup_matrix,
    content_matrix,
    readout_matrix,
    forgetting_narrow_matrix,
    forgetting_widen_matrix,
    forgetting_offset,
    stepsize_narrow_matrix,
    stepsize_widen_matrix,
    stepsize_offset,
    gating_narrow_matrix,
    gating_widen_matrix,
    erasure_lookup_coef,
    lookup_step_fraction,
    diagonal_reward_coef,
    group_layernorm_coef,
):
    highest = lax.Precision.HIGHEST
    segment_length = layer_activation.shape[0]
    stepsize_fraction = query_matrix.shape[1]
    local_attentioners = stepsize_fraction // CHANNELS_PER_ONE
    position = lax.axis_index("seq")
    column = lax.axis_index("tp")
    gathered = lax.all_gather(layer_activation, "tp", axis=1, tiled=True)
    floats = gathered.astype(jnp.float32)
    average = jnp.mean(floats, axis=1, keepdims=True)
    centred = floats - average
    variance = jnp.mean(centred * centred, axis=1, keepdims=True)
    normed = (centred * lax.rsqrt(variance + EPS) * entry_layernorm_coef).astype(jnp.bfloat16)
    normal_f = normed.astype(jnp.float32)
    arrived = from_behind(normed[-1:], "seq", 1)
    bounds = jnp.cumsum(sequence_extents)
    first_token = position * segment_length
    before = first_token - 1
    segment_before = (before >= bounds[0]).astype(jnp.int32) + (before >= bounds[1]).astype(
        jnp.int32
    )
    joined = (segment_before == sequence_label[0]) & (position > 0)
    continues = jnp.concatenate([joined[None], sequence_label[1:] == sequence_label[:-1]])
    previous = jnp.concatenate([arrived.astype(jnp.float32), normal_f[:-1]], axis=0)
    previous = jnp.where(continues[:, None], previous, jnp.zeros_like(previous))
    difference = previous - normal_f

    def blended(which):
        return (normal_f + difference * lagged_blend_coefs[which]).astype(jnp.bfloat16)

    receptance = matmul(blended(0), query_matrix)
    keys = matmul(blended(2), lookup_matrix)
    values = matmul(blended(3), content_matrix)
    decay_hidden = jnp.tanh(matmul(blended(1), forgetting_narrow_matrix)).astype(jnp.bfloat16)
    learn_hidden = matmul(blended(4), stepsize_narrow_matrix).astype(jnp.bfloat16)
    gate_hidden = jax.nn.sigmoid(matmul(blended(5), gating_narrow_matrix)).astype(jnp.bfloat16)
    log_rate = (
        -jax.nn.softplus(-(forgetting_offset + matmul(decay_hidden, forgetting_widen_matrix))) - 0.5
    )
    log_decay = -jnp.exp(log_rate)
    learning = jax.nn.sigmoid(stepsize_offset + matmul(learn_hidden, stepsize_widen_matrix))
    gating_signal = matmul(gate_hidden, gating_widen_matrix)
    removal = (keys * erasure_lookup_coef).reshape(
        segment_length, local_attentioners, CHANNELS_PER_ONE
    )
    removal = removal * lax.rsqrt(jnp.sum(removal * removal, axis=-1, keepdims=True) + 1e-06)
    written = keys * (1.0 + (learning - 1.0) * lookup_step_fraction)
    split_queries = receptance.reshape(segment_length, local_attentioners, CHANNELS_PER_ONE)
    split_lookups = written.reshape(segment_length, local_attentioners, CHANNELS_PER_ONE)
    split_contents = values.reshape(segment_length, local_attentioners, CHANNELS_PER_ONE)
    head_w = log_decay.reshape(segment_length, local_attentioners, CHANNELS_PER_ONE)
    head_a = learning.reshape(segment_length, local_attentioners, CHANNELS_PER_ONE)
    padded_v = jnp.concatenate([split_contents, jnp.zeros_like(split_contents)], axis=-1)
    local_ends = bounds - 1 - first_token
    block_len = min(64, segment_length)
    blocks = segment_length // block_len
    steps_in = jnp.arange(block_len, dtype=jnp.int32)
    strict_lower = steps_in[:, None] > steps_in[None, :]
    with_diag = steps_in[:, None] >= steps_in[None, :]
    unit_eye = jnp.eye(block_len, dtype=jnp.float32)

    def regroup(array):
        return array.reshape((blocks, block_len) + array.shape[1:])

    def block_step(carry, inputs):
        stacked, saved = carry
        block_start, still, r_blk, k_blk, v_blk, n_blk, lw_blk, a_blk = inputs
        restarts = jnp.logical_not(still).astype(jnp.int32)
        epochs = jnp.cumsum(restarts)
        from_start = (epochs == 0).astype(jnp.float32)
        log_total = jnp.cumsum(lw_blk, axis=0)
        query_a = -n_blk * jnp.exp(log_total - lw_blk)
        scaled_beta = n_blk * a_blk * jnp.exp(-log_total)
        scaled_key = k_blk * jnp.exp(-log_total)
        scaled_query = r_blk * jnp.exp(log_total)
        same_run = epochs[:, None] == epochs[None, :]
        strict_mask = (strict_lower & same_run).astype(jnp.float32)
        diag_mask = (with_diag & same_run).astype(jnp.float32)

        def paired(left, right, mask):
            return jnp.einsum("thj,shj->hts", left, right, precision=highest) * mask[None]

        mix_beta = paired(query_a, scaled_beta, strict_mask)
        mix_key = paired(query_a, scaled_key, strict_mask)
        read_beta = paired(scaled_query, scaled_beta, diag_mask)
        read_key = paired(scaled_query, scaled_key, diag_mask)
        from_state = jnp.einsum(
            "thj,hij->hti", query_a * from_start[:, None, None], stacked, precision=highest
        )
        right_side = from_state + jnp.einsum("hts,shi->hti", mix_key, v_blk, precision=highest)
        pseudo = jax.scipy.linalg.solve_triangular(
            unit_eye[None] - mix_beta, right_side, lower=True, unit_diagonal=True
        )
        outputs_blk = jnp.einsum(
            "thj,hij->thi", scaled_query * from_start[:, None, None], stacked, precision=highest
        )
        outputs_blk = outputs_blk + jnp.einsum("hts,hsi->thi", read_beta, pseudo, precision=highest)
        outputs_blk = outputs_blk + jnp.einsum("hts,shi->thi", read_key, v_blk, precision=highest)

        def state_at(moment):
            growth = jnp.exp(lax.dynamic_index_in_dim(log_total, moment, 0, keepdims=False))
            epoch_now = lax.dynamic_index_in_dim(epochs, moment, 0, keepdims=False)
            chosen = ((steps_in <= moment) & (epochs == epoch_now)).astype(jnp.float32)
            weight_beta = scaled_beta * chosen[:, None, None] * growth[None]
            weight_key = scaled_key * chosen[:, None, None] * growth[None]
            start_part = stacked * (growth * (epoch_now == 0).astype(jnp.float32))[:, None, :]
            result = start_part + jnp.einsum("hsi,shj->hij", pseudo, weight_beta, precision=highest)
            return result + jnp.einsum("shi,shj->hij", v_blk, weight_key, precision=highest)

        new_stacked = state_at(jnp.int32(block_len - 1))
        updated = []
        for prompt in range(PROMPTS):
            offset_end = local_ends[prompt] - block_start
            inside = (offset_end >= 0) & (offset_end < block_len)
            moment = jnp.clip(offset_end, 0, block_len - 1)
            updated.append(jnp.where(inside, state_at(moment), saved[prompt]))
        return ((new_stacked, jnp.stack(updated)), outputs_blk)

    identity = jnp.broadcast_to(
        jnp.eye(CHANNELS_PER_ONE, dtype=jnp.float32),
        (local_attentioners, CHANNELS_PER_ONE, CHANNELS_PER_ONE),
    )
    start_stack = jnp.concatenate([jnp.zeros_like(identity), identity], axis=1)
    start_saved = jnp.zeros(
        (PROMPTS, local_attentioners, 2 * CHANNELS_PER_ONE, CHANNELS_PER_ONE), jnp.float32
    )
    block_starts = jnp.arange(blocks, dtype=jnp.int32) * block_len
    scan_inputs = (
        block_starts,
        regroup(continues),
        regroup(split_queries),
        regroup(split_lookups),
        regroup(padded_v),
        regroup(removal),
        regroup(head_w),
        regroup(head_a),
    )
    (final_stack, saved), grouped_out = lax.scan(
        block_step, (start_stack, start_saved), scan_inputs
    )
    outputs = grouped_out.reshape(segment_length, local_attentioners, 2 * CHANNELS_PER_ONE)
    local_state = final_stack[:, :CHANNELS_PER_ONE]
    transition = final_stack[:, CHANNELS_PER_ONE:]

    def passing(turn, incoming):
        return from_behind(
            (compose(incoming, transition) + local_state).astype(jnp.bfloat16), "seq", 1
        ).astype(jnp.float32)

    state_in = lax.fori_loop(0, lax.axis_size("seq") - 1, passing, jnp.zeros_like(local_state))
    readout = outputs[:, :, :CHANNELS_PER_ONE] + jnp.einsum(
        "hij,thj->thi", state_in, outputs[:, :, CHANNELS_PER_ONE:], precision=highest
    )
    centre = readout - jnp.mean(readout, axis=-1, keepdims=True)
    spread = jnp.mean(centre * centre, axis=-1, keepdims=True)
    group_standardized = (
        centre
        * lax.rsqrt(spread + GROUP_EPS)
        * group_layernorm_coef.reshape(local_attentioners, CHANNELS_PER_ONE)
    )
    diagonal_reward = (
        jnp.sum(
            split_queries
            * split_lookups
            * diagonal_reward_coef.reshape(local_attentioners, CHANNELS_PER_ONE),
            axis=-1,
            keepdims=True,
        )
        * split_contents
    )
    visible_entries = (
        (group_standardized + diagonal_reward).reshape(segment_length, stepsize_fraction)
        * gating_signal
    ).astype(jnp.bfloat16)
    partial_value = matmul(visible_entries, readout_matrix)
    summed = lax.psum_scatter(
        partial_value.astype(jnp.bfloat16), "tp", scatter_dimension=1, tiled=True
    ).astype(jnp.float32)
    mixed = (summed + layer_activation.astype(jnp.float32)).astype(jnp.bfloat16)
    final_states = jnp.zeros(
        (1, local_attentioners, CHANNELS_PER_ONE, CHANNELS_PER_ONE), jnp.float32
    )
    final_rows = jnp.zeros((1, stepsize_fraction), jnp.bfloat16)
    for prompt in range(PROMPTS):
        last_token = bounds[prompt] - 1
        holder = last_token // segment_length
        inside = jnp.clip(last_token - first_token, 0, segment_length - 1)
        recorded = saved[prompt]
        state_end = (
            compose(state_in, recorded[:, CHANNELS_PER_ONE:]) + recorded[:, :CHANNELS_PER_ONE]
        )
        row_end = lax.dynamic_slice(
            normal_f, (inside, column * stepsize_fraction), (1, stepsize_fraction)
        )
        got_state, got_row = (
            broadcast(state_end.astype(jnp.bfloat16), "seq", holder).astype(state_end.dtype),
            broadcast(row_end.astype(jnp.bfloat16), "seq", holder).astype(row_end.dtype),
        )
        is_owner = position == destination_slots[prompt]
        final_states = jnp.where(is_owner, got_state[None], final_states)
        final_rows = jnp.where(is_owner, got_row.astype(jnp.bfloat16), final_rows)
    return (mixed, final_states, final_rows)


def solution(mesh):
    return jax.shard_map(
        on_device,
        mesh=mesh,
        in_specs=(
            P("seq", "tp"),
            P("seq"),
            P(),
            P(),
            P(),
            P(),
            P(None, "tp"),
            P(None, "tp"),
            P(None, "tp"),
            P("tp", None),
            P(),
            P(None, "tp"),
            P("tp"),
            P(),
            P(None, "tp"),
            P("tp"),
            P(),
            P(None, "tp"),
            P("tp"),
            P("tp"),
            P("tp"),
            P("tp"),
        ),
        out_specs=(P("seq", "tp"), P("seq", "tp", None, None), P("seq", "tp")),
        check_vma=False,
    )
```

profile of v0, /device:TPU:0, one launch (start us, length us, event | category | flops | bytes accessed | tf_op | source)
XLA Modules:
  0.0 698.0 jit_solution(5239069506846674704)
XLA Ops:
  14.6 17.4 %all-gather.2.cloned.1.call-done = bf16[384,2048]{1,0:T(8,128)(2,1)} async-done(((bf16[384,512]{1,0:T(8,128)(2,1)}), bf16[384,2048]{1,0:T(8,128)(2,1)}) %all-gather.2.cloned.1.call-update) | async-done | bytes 1572880 | tf_op jit(solution)/shard_map/all_gather | solution.py:61
  37.5 3.4 collective-permute-start.1
  42.8 3.5 slice.133
  46.3 3.9 fusion.101
  51.7 5.1 fusion.72
  59.3 5.5 fusion.149
  68.7 5.1 fusion.139
  80.6 4.5 fusion.74
  92.1 414.9 %while.27 = (s32[]{:T(128)}, f32[8,128,64]{1,2,0:T(8,128)S(1)}, f32[2,8,128,64]{2,3,1,0:T(8,128)}, f32[6,64,8,128]{3,2,1,0:T(8,128)}, f32[6,64,8,64]{3,2,1,0:T(8...) while((s32[]{:T(128)}, f32[8,128,64]{1,2,0:T(8,128)S(1)}, ...), condition=%wide.region_7.8_spmd.clone.clone, body=%wide.region_4.7_spmd.clone.clone.sunk | while | flops 708762112 | bytes 20262212 | solution.py:191
  108.9 40.7 %custom-call.9 = f32[8,1,64,64]{2,3,1,0:T(8,128)} custom-call(f32[8,1,64,64]{3,2,1,0:T(8,128)} %fusion.259), custom_call_target="InvertDiagBlocksLowerTriangular" | custom-call | tf_op jit(solution)/shard_map/while/body/eval_jaxpr/jit(_solve_triangular)/vmap()/triangular_solve | solution.py:144
  178.1 40.7 %custom-call.9 = f32[8,1,64,64]{2,3,1,0:T(8,128)} custom-call(f32[8,1,64,64]{3,2,1,0:T(8,128)} %fusion.259), custom_call_target="InvertDiagBlocksLowerTriangular" | custom-call | tf_op jit(solution)/shard_map/while/body/eval_jaxpr/jit(_solve_triangular)/vmap()/triangular_solve | solution.py:144
  247.2 40.7 %custom-call.9 = f32[8,1,64,64]{2,3,1,0:T(8,128)} custom-call(f32[8,1,64,64]{3,2,1,0:T(8,128)} %fusion.259), custom_call_target="InvertDiagBlocksLowerTriangular" | custom-call | tf_op jit(solution)/shard_map/while/body/eval_jaxpr/jit(_solve_triangular)/vmap()/triangular_solve | solution.py:144
  316.4 40.7 %custom-call.9 = f32[8,1,64,64]{2,3,1,0:T(8,128)} custom-call(f32[8,1,64,64]{3,2,1,0:T(8,128)} %fusion.259), custom_call_target="InvertDiagBlocksLowerTriangular" | custom-call | tf_op jit(solution)/shard_map/while/body/eval_jaxpr/jit(_solve_triangular)/vmap()/triangular_solve | solution.py:144
  385.5 40.7 %custom-call.9 = f32[8,1,64,64]{2,3,1,0:T(8,128)} custom-call(f32[8,1,64,64]{3,2,1,0:T(8,128)} %fusion.259), custom_call_target="InvertDiagBlocksLowerTriangular" | custom-call | tf_op jit(solution)/shard_map/while/body/eval_jaxpr/jit(_solve_triangular)/vmap()/triangular_solve | solution.py:144
  454.7 40.7 %custom-call.9 = f32[8,1,64,64]{2,3,1,0:T(8,128)} custom-call(f32[8,1,64,64]{3,2,1,0:T(8,128)} %fusion.259), custom_call_target="InvertDiagBlocksLowerTriangular" | custom-call | tf_op jit(solution)/shard_map/while/body/eval_jaxpr/jit(_solve_triangular)/vmap()/triangular_solve | solution.py:144
  514.2 2.8 copy.135
  517.1 55.1 %while.28 = (s32[]{:T(128)}, f32[8,64,64]{2,1,0:T(8,128)S(1)}, f32[8,64,64]{2,1,0:T(8,128)S(1)}, f32[8,64,64]{2,1,0:T(8,128)S(1)}, s32[]{:T(128)}, /*index=5*/s32[]{:T(128)}) while((s32[]{:T(128)}, f32[8,64,64]{2,1,0:T(8,128)S(1)}, f32[8,64,64]{2,1,0:T(8,128)S(1)}, f32[8,64,64]{2,1,0:T(8,128)S(1)}, s32[]{:T(128)}, ...), condition=%wide.region_9.10_spmd.clone, body=%wide.region_8.9_spmd.clone.sunk | while | flops 25296900 | bytes 917623 | solution.py:203
  517.4 3.4 collective-permute-start
  520.8 2.8 collective-permute-done
  524.1 4.4 collective-permute-start
  531.4 4.4 collective-permute-start
  538.7 5.2 collective-permute-start
  546.9 5.3 collective-permute-start
  555.1 5.3 collective-permute-start
  560.3 3.0 collective-permute-done
  563.8 5.6 collective-permute-start
  572.1 4.1 fusion.157
  579.0 4.4 fusion.116
  585.6 4.1 convolution_convert_fusion
  592.5 22.7 %all-reduce.2 = (bf16[1,512]{1,0:T(2,128)(2,1)S(1)}, bf16[1,512]{1,0:T(2,128)(2,1)S(1)}) all-reduce(bf16[1,512]{1,0:T(2,128)(2,1)S(1)} %get-tuple-element.333, bf16[1,512]{1,0:T(2,128)(2,1)S(1)} %get-tuple-element.332), channel_id=1, replica_groups=mesh['seq'=8,'tp'=4] {'seq'}, use_global_device_ids=true, to_apply=%region_16.17 | all-reduce | flops 1024 | bytes 4096 | tf_op jit(solution)/shard_map/psum | solution.py:20
  615.9 43.6 %all-reduce.6.cloned.1.call-done = (bf16[8,64,64]{2,1,0:T(8,128)(2,1)}, bf16[8,64,64]{2,1,0:T(8,128)(2,1)}) async-done(((bf16[8,64,64]{2,1,0:T(8,128)(2,1)}, bf16[8,64,64]{2,1,0:T(8,128)(2,1)}), (bf16[8,64,64]{2,1,0:T(8,128)(2,1)}, bf16[8,64,64]{2,1,0:T(8,128)(2,1)})) %all-reduce.6.cloned.1.call-update) | async-done | bytes 131088 | tf_op jit(solution)/shard_map/psum | solution.py:20
  661.1 28.5 %reduce-scatter.2.cloned.1.call-done = bf16[384,512]{1,0:T(8,128)(2,1)} async-done(((bf16[384,2048]{1,0:T(8,128)(2,1)}), bf16[384,512]{1,0:T(8,128)(2,1)}) %reduce-scatter.2.cloned.1.call-update) | async-done | bytes 393232 | tf_op jit(solution)/shard_map/reduce_scatter | solution.py:229
  (352 shorter events, 207.8 us)
Async XLA Ops:
  7.2 52.1 %copy-start = (bf16[2048,512]{1,0:T(8,128)(2,1)S(1)}, bf16[2048,512]{1,0:T(8,128)(2,1)}, u32[]{:S(2)}) copy-start(bf16[2048,512]{1,0:T(8,128)(2,1)} %param.33) | copy-start | bytes 6291460
  7.2 28.6 %copy-start.15 = (f32[2048]{0:T(1024)S(1)}, f32[2048]{0:T(1024)}, u32[]{:S(2)}) copy-start(f32[2048]{0:T(1024)} %param.30) | copy-start | bytes 24580
  7.2 24.8 %all-gather.2.cloned.1.call-start = ((), (), s32[]{:S(2)}) async-start(), calls=%async_computation.1 | async-start | bytes 1966080 | tf_op jit(solution)/shard_map/all_gather | solution.py:61
  7.9 651.5 %all-reduce.6.cloned.1.call-start = ((), (), s32[]{:S(2)}) async-start(), calls=%async_computation.3 | async-start | bytes 524288 | tf_op jit(solution)/shard_map/psum | solution.py:20
  14.6 27.9 %copy-start.16 = (f32[512]{0:T(512)S(1)}, f32[512]{0:T(512)}, u32[]{:S(2)}) copy-start(f32[512]{0:T(512)} %param.46) | copy-start | bytes 6148
  14.6 28.0 %copy-start.17 = (f32[512]{0:T(512)S(1)}, f32[512]{0:T(512)}, u32[]{:S(2)}) copy-start(f32[512]{0:T(512)} %param.47) | copy-start | bytes 6148
  37.5 8.7 %collective-permute-start.1 = (bf16[1,2048]{1,0:T(2,128)(2,1)S(1)}, bf16[1,2048]{1,0:T(2,128)(2,1)S(1)}, u32[]{:S(2)}, u32[]{:S(2)}) collective-permute-start(bf16[1,2048]{1,0:T(2,128)(2,1)S(1)} %slice.132), channel_id=1, source_target_pairs={{0,4},{4,8},{8,12},{12,16},{16,20},{20,24},{24,28},{1,5},{5,9},{9,... | collective-permute-start | bytes 12296 | tf_op jit(solution)/shard_map/ppermute | solution.py:15
  51.7 7.6 %copy-start.21 = (f32[512]{0:T(512)S(1)}, f32[512]{0:T(512)}, u32[]{:S(2)}) copy-start(f32[512]{0:T(512)} %param.44) | copy-start | bytes 6148
  51.7 7.6 %copy-start.22 = (f32[512]{0:T(512)S(1)}, f32[512]{0:T(512)}, u32[]{:S(2)}) copy-start(f32[512]{0:T(512)} %param.45) | copy-start | bytes 6148
  73.8 5.3 copy-start.14
  85.1 6.1 copy-start.9
  149.6 4.9 copy-start.1
  218.7 4.9 copy-start.1
  287.9 4.9 copy-start.1
  357.1 4.9 copy-start.1
  426.2 4.9 copy-start.1
  495.4 4.9 copy-start.1
  512.1 4.9 copy-start.3
  517.4 6.2 collective-permute-start
  524.1 6.9 collective-permute-start
  531.4 6.9 collective-permute-start
  538.7 7.7 %collective-permute-start = (bf16[8,64,64]{2,1,0:T(8,128)(2,1)S(1)}, bf16[8,64,64]{2,1,0:T(8,128)(2,1)S(1)}, u32[]{:S(2)}, u32[]{:S(2)}) collective-permute-start(bf16[8,64,64]{2,1,0:T(8,128)(2,1)S(1)} %fusion.267), channel_id=1, source_target_pairs={{0,4},{4,8},{8,12},{12,16},{16,20},{20,24},{24,28},{1,5},{5,9},{9,... | collective-permute-start | bytes 196616 | tf_op jit(solution)/shard_map/while/body/eval_jaxpr/ppermute | solution.py:15
  546.9 7.8 %collective-permute-start = (bf16[8,64,64]{2,1,0:T(8,128)(2,1)S(1)}, bf16[8,64,64]{2,1,0:T(8,128)(2,1)S(1)}, u32[]{:S(2)}, u32[]{:S(2)}) collective-permute-start(bf16[8,64,64]{2,1,0:T(8,128)(2,1)S(1)} %fusion.267), channel_id=1, source_target_pairs={{0,4},{4,8},{8,12},{12,16},{16,20},{20,24},{24,28},{1,5},{5,9},{9,... | collective-permute-start | bytes 196616 | tf_op jit(solution)/shard_map/while/body/eval_jaxpr/ppermute | solution.py:15
  555.1 8.3 %collective-permute-start = (bf16[8,64,64]{2,1,0:T(8,128)(2,1)S(1)}, bf16[8,64,64]{2,1,0:T(8,128)(2,1)S(1)}, u32[]{:S(2)}, u32[]{:S(2)}) collective-permute-start(bf16[8,64,64]{2,1,0:T(8,128)(2,1)S(1)} %fusion.267), channel_id=1, source_target_pairs={{0,4},{4,8},{8,12},{12,16},{16,20},{20,24},{24,28},{1,5},{5,9},{9,... | collective-permute-start | bytes 196616 | tf_op jit(solution)/shard_map/while/body/eval_jaxpr/ppermute | solution.py:15
  563.8 8.1 %collective-permute-start = (bf16[8,64,64]{2,1,0:T(8,128)(2,1)S(1)}, bf16[8,64,64]{2,1,0:T(8,128)(2,1)S(1)}, u32[]{:S(2)}, u32[]{:S(2)}) collective-permute-start(bf16[8,64,64]{2,1,0:T(8,128)(2,1)S(1)} %fusion.267), channel_id=1, source_target_pairs={{0,4},{4,8},{8,12},{12,16},{16,20},{20,24},{24,28},{1,5},{5,9},{9,... | collective-permute-start | bytes 196616 | tf_op jit(solution)/shard_map/while/body/eval_jaxpr/ppermute | solution.py:15
  572.1 4.3 copy-start.8
  572.1 4.3 copy-start.10
  579.0 4.4 copy-start.13
  579.0 5.5 copy-start.12
  585.6 4.2 copy-start.18
  585.6 104.1 %copy-start.11 = (bf16[384,512]{1,0:T(8,128)(2,1)S(1)}, bf16[384,512]{1,0:T(8,128)(2,1)}, u32[]{:S(2)}) copy-start(bf16[384,512]{1,0:T(8,128)(2,1)} %param.26) | copy-start | bytes 1179652
  585.6 104.0 %reduce-scatter.2.cloned.1.call-start = ((), (), s32[]{:S(2)}) async-start(), calls=%async_computation.2 | async-start | bytes 1966080 | tf_op jit(solution)/shard_map/reduce_scatter | solution.py:229
  (13 other events, 38.1 us)
Sparse Core Ops, SparseCore 0:
  9.6 22.3 all-gather.1
  585.7 73.6 all-reduce.5
  662.1 27.4 reduce-scatter.1
where the time goes:
time: 701 us; the launch traced here: 698 us
  other arithmetic  299 us (43%)
  matrix products  120 us (17%)
  waiting for transfers between devices  109 us (16%)
  local copies, waits for them, and re-layouts  62.6 us (9%)
  starting transfers between devices  36.9 us (5%)
  loops' own time  29.5 us (4%)
  blocking collectives  22.7 us (3%)
  between operations  18.8 us (3%)
    another operation x18, other arithmetic, block_step(): jax.scipy.linalg.solve_triangular(unit_eye[None] - mix_beta, right_side,...  245 us
    psum x1, waiting for transfers between devices, broadcast(): return lax.psum(kept, axis)  43.6 us
    ppermute x8, starting transfers between devices, from_behind(): return lax.ppermute(array, axis, pairs)  36.8 us
    dot_general x7, matrix products, matmul(): return jnp.dot(left, right, preferred_element_type=jnp.float32)  32.6 us
    another operation x1, loops' own time, on_device(): lax.scan(block_step, (start_stack, start_saved), scan_inputs)  29.1 us
    reduce_scatter x1, waiting for transfers between devices, on_device(): lax.psum_scatter(partial_value.astype(jnp.bfloat16), 'tp', scatter_dimens...  28.5 us
    psum x1, blocking collectives, broadcast(): return lax.psum(kept, axis)  22.7 us
    dot_general x24, matrix products, paired(): jnp.einsum('thj,shj->hts', left, right, precision=highest) * mask[None]  18.6 us
  transfers between devices with their start and end apart: 11, of which 10 were waited for; matrix products, arithmetic and copies ran while one was open for 2% of the time, Pallas kernels for 0%

commit v1 on v0

--- a/solution.py
+++ b/solution.py
@@ -58,7 +58,12 @@
     local_attentioners = stepsize_fraction // CHANNELS_PER_ONE
     position = lax.axis_index("seq")
     column = lax.axis_index("tp")
-    gathered = lax.all_gather(layer_activation, "tp", axis=1, tiled=True)
+    ring = [layer_activation]
+    for hop in range(3):
+        ring.append(lax.ppermute(ring[-1], "tp", [(dev, (dev + 1) % 4) for dev in range(4)]))
+    gathered = jnp.roll(
+        jnp.concatenate(ring[::-1], axis=1), (lax.axis_index("tp") + 1) * ring[0].shape[1], axis=1
+    )
     floats = gathered.astype(jnp.float32)
     average = jnp.mean(floats, axis=1, keepdims=True)
     centred = floats - average

time: 701 us -> 671 us (0.957)
  waiting for transfers between devices: 109 us -> 78.4 us
    reduce_scatter x1, waiting for transfers between devices: 28.5 us -> 0.01 us  [on_device(): lax.psum_scatter(partial_value.astype(jnp.bfloat16), 'tp', scatter_dimens...]
    all_gather x1 -> x0, waiting for transfers between devices: 17.4 us -> none  [on_device(): gathered = lax.all_gather(layer_activation, 'tp', axis=1, tiled=True)]
    ppermute x0 -> x3, waiting for transfers between devices: none -> 14.7 us  [on_device(): lax.ppermute(ring[-1], 'tp', [(dev, (dev + 1) % 4) for dev in range(4)])]
  transfers between devices with their start and end apart: 11 -> 13, of which waited for: 10 -> 11; matrix products, arithmetic and copies ran while one was open for 2% -> 3% of each run, Pallas kernels for 0% -> 0%
where the time goes in v1:
time: 671 us; the launch traced here: 668 us
  other arithmetic  296 us (44%)
  matrix products  120 us (18%)
  waiting for transfers between devices  78.4 us (12%)
  local copies, waits for them, and re-layouts  64 us (10%)
  starting transfers between devices  38.3 us (6%)
  loops' own time  28.1 us (4%)
  blocking collectives  22.9 us (3%)
  between operations  20.6 us (3%)
    another operation x18, other arithmetic, block_step(): jax.scipy.linalg.solve_triangular(unit_eye[None] - mix_beta, right_side,...  245 us
    psum x1, waiting for transfers between devices, broadcast(): return lax.psum(kept, axis)  44.5 us
    ppermute x8, starting transfers between devices, from_behind(): return lax.ppermute(array, axis, pairs)  37.5 us
    dot_general x7, matrix products, matmul(): return jnp.dot(left, right, preferred_element_type=jnp.float32)  32.6 us
    another operation x1, loops' own time, on_device(): lax.scan(block_step, (start_stack, start_saved), scan_inputs)  27.6 us
    psum x1, blocking collectives, broadcast(): return lax.psum(kept, axis)  22.9 us
    ppermute x8, waiting for transfers between devices, from_behind(): return lax.ppermute(array, axis, pairs)  19.1 us
    dot_general x24, matrix products, paired(): jnp.einsum('thj,shj->hts', left, right, precision=highest) * mask[None]  18.6 us
  transfers between devices with their start and end apart: 13, of which 11 were waited for; matrix products, arithmetic and copies ran while one was open for 3% of the time, Pallas kernels for 0%

profile of v1, /device:TPU:0, one launch (start us, length us, event | category | flops | bytes accessed | tf_op | source)
XLA Modules:
  0.0 668.5 jit_solution(13469214140270125074)
XLA Ops:
  17.2 6.2 collective-permute-done.2
  24.5 6.1 collective-permute-done.3
  34.6 4.4 collective-permute-start.4
  41.5 3.4 slice.133
  45.0 3.9 fusion.101
  50.4 5.1 fusion.72
  58.0 5.5 fusion.149
  67.5 5.1 fusion.139
  79.4 4.5 fusion.74
  91.0 412.5 %while.27 = (s32[]{:T(128)}, f32[8,128,64]{1,2,0:T(8,128)S(1)}, f32[2,8,128,64]{2,3,1,0:T(8,128)}, f32[6,64,8,128]{3,2,1,0:T(8,128)}, f32[6,64,8,64]{3,2,1,0:T(8...) while((s32[]{:T(128)}, f32[8,128,64]{1,2,0:T(8,128)S(1)}, ...), condition=%wide.region_7.8_spmd.clone.clone, body=%wide.region_4.7_spmd.clone.clone.sunk | while | flops 708762112 | bytes 20262212 | solution.py:196
  107.3 40.7 %custom-call.11 = f32[8,1,64,64]{2,3,1,0:T(8,128)} custom-call(f32[8,1,64,64]{3,2,1,0:T(8,128)} %fusion.259), custom_call_target="InvertDiagBlocksLowerTriangular" | custom-call | tf_op jit(solution)/shard_map/while/body/eval_jaxpr/jit(_solve_triangular)/vmap()/triangular_solve | solution.py:149
  176.1 40.7 %custom-call.11 = f32[8,1,64,64]{2,3,1,0:T(8,128)} custom-call(f32[8,1,64,64]{3,2,1,0:T(8,128)} %fusion.259), custom_call_target="InvertDiagBlocksLowerTriangular" | custom-call | tf_op jit(solution)/shard_map/while/body/eval_jaxpr/jit(_solve_triangular)/vmap()/triangular_solve | solution.py:149
  244.8 40.7 %custom-call.11 = f32[8,1,64,64]{2,3,1,0:T(8,128)} custom-call(f32[8,1,64,64]{3,2,1,0:T(8,128)} %fusion.259), custom_call_target="InvertDiagBlocksLowerTriangular" | custom-call | tf_op jit(solution)/shard_map/while/body/eval_jaxpr/jit(_solve_triangular)/vmap()/triangular_solve | solution.py:149
  313.5 40.7 %custom-call.11 = f32[8,1,64,64]{2,3,1,0:T(8,128)} custom-call(f32[8,1,64,64]{3,2,1,0:T(8,128)} %fusion.259), custom_call_target="InvertDiagBlocksLowerTriangular" | custom-call | tf_op jit(solution)/shard_map/while/body/eval_jaxpr/jit(_solve_triangular)/vmap()/triangular_solve | solution.py:149
  382.3 40.7 %custom-call.11 = f32[8,1,64,64]{2,3,1,0:T(8,128)} custom-call(f32[8,1,64,64]{3,2,1,0:T(8,128)} %fusion.259), custom_call_target="InvertDiagBlocksLowerTriangular" | custom-call | tf_op jit(solution)/shard_map/while/body/eval_jaxpr/jit(_solve_triangular)/vmap()/triangular_solve | solution.py:149
  451.0 40.7 %custom-call.11 = f32[8,1,64,64]{2,3,1,0:T(8,128)} custom-call(f32[8,1,64,64]{3,2,1,0:T(8,128)} %fusion.259), custom_call_target="InvertDiagBlocksLowerTriangular" | custom-call | tf_op jit(solution)/shard_map/while/body/eval_jaxpr/jit(_solve_triangular)/vmap()/triangular_solve | solution.py:149
  510.6 2.8 copy.135
  513.5 55.6 %while.28 = (s32[]{:T(128)}, f32[8,64,64]{2,1,0:T(8,128)S(1)}, f32[8,64,64]{2,1,0:T(8,128)S(1)}, f32[8,64,64]{2,1,0:T(8,128)S(1)}, s32[]{:T(128)}, /*index=5*/s32[]{:T(128)}) while((s32[]{:T(128)}, f32[8,64,64]{2,1,0:T(8,128)S(1)}, f32[8,64,64]{2,1,0:T(8,128)S(1)}, f32[8,64,64]{2,1,0:T(8,128)S(1)}, s32[]{:T(128)}, ...), condition=%wide.region_9.10_spmd.clone, body=%wide.region_8.9_spmd.clone.sunk | while | flops 25296900 | bytes 917623 | solution.py:208
  513.9 3.4 collective-permute-start
  520.2 4.4 collective-permute-start
  527.5 4.4 collective-permute-start
  534.8 5.2 collective-permute-start
  543.0 5.3 collective-permute-start
  548.3 3.3 collective-permute-done
  552.0 5.5 collective-permute-start
  557.5 3.3 collective-permute-done
  561.3 5.0 collective-permute-start
  569.1 4.1 fusion.157
  576.0 4.4 fusion.116
  582.6 4.0 convolution_convert_fusion
  589.5 22.9 %all-reduce.2 = (bf16[1,512]{1,0:T(2,128)(2,1)S(1)}, bf16[1,512]{1,0:T(2,128)(2,1)S(1)}) all-reduce(bf16[1,512]{1,0:T(2,128)(2,1)S(1)} %get-tuple-element.333, bf16[1,512]{1,0:T(2,128)(2,1)S(1)} %get-tuple-element.332), channel_id=1, replica_groups=mesh['seq'=8,'tp'=4] {'seq'}, use_global_device_ids=true, to_apply=%region_16.17 | all-reduce | flops 1024 | bytes 4096 | tf_op jit(solution)/shard_map/psum | solution.py:20
  613.0 44.5 %all-reduce.6.cloned.1.call-done = (bf16[8,64,64]{2,1,0:T(8,128)(2,1)}, bf16[8,64,64]{2,1,0:T(8,128)(2,1)}) async-done(((bf16[8,64,64]{2,1,0:T(8,128)(2,1)}, bf16[8,64,64]{2,1,0:T(8,128)(2,1)}), (bf16[8,64,64]{2,1,0:T(8,128)(2,1)}, bf16[8,64,64]{2,1,0:T(8,128)(2,1)})) %all-reduce.6.cloned.1.call-update) | async-done | bytes 131088 | tf_op jit(solution)/shard_map/psum | solution.py:20
  (377 shorter events, 208.8 us)
Async XLA Ops:
  8.0 50.0 %copy-start = (bf16[2048,512]{1,0:T(8,128)(2,1)S(1)}, bf16[2048,512]{1,0:T(8,128)(2,1)}, u32[]{:S(2)}) copy-start(bf16[2048,512]{1,0:T(8,128)(2,1)} %param.33) | copy-start | bytes 6291460
  8.0 23.9 %copy-start.7 = (bf16[384,512]{1,0:T(8,128)(2,1)S(1)}, bf16[384,512]{1,0:T(8,128)(2,1)}, u32[]{:S(2)}) copy-start(bf16[384,512]{1,0:T(8,128)(2,1)} %param.26) | copy-start | bytes 1179652
  8.0 649.5 %all-reduce.6.cloned.1.call-start = ((), (), s32[]{:S(2)}) async-start(), calls=%async_computation.2 | async-start | bytes 524288 | tf_op jit(solution)/shard_map/psum | solution.py:20
  8.1 8.1 %collective-permute-start.1 = (bf16[384,512]{1,0:T(8,128)(2,1)}, bf16[384,512]{1,0:T(8,128)(2,1)S(1)}, u32[]{:S(2)}, u32[]{:S(2)}) collective-permute-start(bf16[384,512]{1,0:T(8,128)(2,1)} %param.26), channel_id=1, source_target_pairs={{0,1},{1,2},{2,3},{3,0},{4,5},{5,6},{6,7},{7,4},{8,9},{9,10},{10,1... | collective-permute-start | bytes 1179656 | tf_op jit(solution)/shard_map/ppermute | solution.py:63
  16.2 7.2 %collective-permute-start.2 = (bf16[384,512]{1,0:T(8,128)(2,1)S(1)}, bf16[384,512]{1,0:T(8,128)(2,1)S(1)}, u32[]{:S(2)}, u32[]{:S(2)}) collective-permute-start(bf16[384,512]{1,0:T(8,128)(2,1)S(1)} %collective-permute-done.1), channel_id=1, source_target_pairs={{0,1},{1,2},{2,3},{3,0},{4,5},{5,6},{6,7},{7,4},{8,9},{9,10},{10,1... | collective-permute-start | bytes 1179656 | tf_op jit(solution)/shard_map/ppermute | solution.py:63
  23.4 7.2 %collective-permute-start.3 = (bf16[384,512]{1,0:T(8,128)(2,1)S(1)}, bf16[384,512]{1,0:T(8,128)(2,1)S(1)}, u32[]{:S(2)}, u32[]{:S(2)}) collective-permute-start(bf16[384,512]{1,0:T(8,128)(2,1)S(1)} %collective-permute-done.2), channel_id=1, source_target_pairs={{0,1},{1,2},{2,3},{3,0},{4,5},{5,6},{6,7},{7,4},{8,9},{9,10},{10,1... | collective-permute-start | bytes 1179656 | tf_op jit(solution)/shard_map/ppermute | solution.py:63
  32.0 9.2 %copy-start.17 = (f32[512]{0:T(512)S(1)}, f32[512]{0:T(512)}, u32[]{:S(2)}) copy-start(f32[512]{0:T(512)} %param.46) | copy-start | bytes 6148
  32.0 9.2 %copy-start.18 = (f32[512]{0:T(512)S(1)}, f32[512]{0:T(512)}, u32[]{:S(2)}) copy-start(f32[512]{0:T(512)} %param.47) | copy-start | bytes 6148
  34.6 10.3 %collective-permute-start.4 = (bf16[1,2048]{1,0:T(2,128)(2,1)S(1)}, bf16[1,2048]{1,0:T(2,128)(2,1)S(1)}, u32[]{:S(2)}, u32[]{:S(2)}) collective-permute-start(bf16[1,2048]{1,0:T(2,128)(2,1)S(1)} %slice.132), channel_id=1, source_target_pairs={{0,4},{4,8},{8,12},{12,16},{16,20},{20,24},{24,28},{1,5},{5,9},{9,... | collective-permute-start | bytes 12296 | tf_op jit(solution)/shard_map/ppermute | solution.py:15
  39.1 18.9 %copy-start.27 = (pred[384]{0:T(512)(128)(4,1)}, pred[384]{0:T(512)(128)(4,1)S(1)}, u32[]{:S(2)}) copy-start(pred[384]{0:T(512)(128)(4,1)S(1)} %pad_add_fusion) | copy-start | bytes 1156
  50.4 7.6 %copy-start.23 = (f32[512]{0:T(512)S(1)}, f32[512]{0:T(512)}, u32[]{:S(2)}) copy-start(f32[512]{0:T(512)} %param.44) | copy-start | bytes 6148
  50.4 7.6 %copy-start.24 = (f32[512]{0:T(512)S(1)}, f32[512]{0:T(512)}, u32[]{:S(2)}) copy-start(f32[512]{0:T(512)} %param.45) | copy-start | bytes 6148
  72.6 5.3 copy-start.14
  83.9 6.1 copy-start.10
  85.6 5.4 copy-start.26
  85.6 5.4 copy-start.30
  216.7 4.9 copy-start.1
  285.5 4.9 copy-start.1
  354.2 4.9 copy-start.1
  491.7 4.9 copy-start.1
  508.5 5.0 copy-start.3
  513.9 5.9 collective-permute-start
  520.2 6.9 %collective-permute-start = (bf16[8,64,64]{2,1,0:T(8,128)(2,1)S(1)}, bf16[8,64,64]{2,1,0:T(8,128)(2,1)S(1)}, u32[]{:S(2)}, u32[]{:S(2)}) collective-permute-start(bf16[8,64,64]{2,1,0:T(8,128)(2,1)S(1)} %fusion.267), channel_id=1, source_target_pairs={{0,4},{4,8},{8,12},{12,16},{16,20},{20,24},{24,28},{1,5},{5,9},{9,... | collective-permute-start | bytes 196616 | tf_op jit(solution)/shard_map/while/body/eval_jaxpr/ppermute | solution.py:15
  527.5 6.9 %collective-permute-start = (bf16[8,64,64]{2,1,0:T(8,128)(2,1)S(1)}, bf16[8,64,64]{2,1,0:T(8,128)(2,1)S(1)}, u32[]{:S(2)}, u32[]{:S(2)}) collective-permute-start(bf16[8,64,64]{2,1,0:T(8,128)(2,1)S(1)} %fusion.267), channel_id=1, source_target_pairs={{0,4},{4,8},{8,12},{12,16},{16,20},{20,24},{24,28},{1,5},{5,9},{9,... | collective-permute-start | bytes 196616 | tf_op jit(solution)/shard_map/while/body/eval_jaxpr/ppermute | solution.py:15
  534.8 7.7 %collective-permute-start = (bf16[8,64,64]{2,1,0:T(8,128)(2,1)S(1)}, bf16[8,64,64]{2,1,0:T(8,128)(2,1)S(1)}, u32[]{:S(2)}, u32[]{:S(2)}) collective-permute-start(bf16[8,64,64]{2,1,0:T(8,128)(2,1)S(1)} %fusion.267), channel_id=1, source_target_pairs={{0,4},{4,8},{8,12},{12,16},{16,20},{20,24},{24,28},{1,5},{5,9},{9,... | collective-permute-start | bytes 196616 | tf_op jit(solution)/shard_map/while/body/eval_jaxpr/ppermute | solution.py:15
  543.0 8.6 %collective-permute-start = (bf16[8,64,64]{2,1,0:T(8,128)(2,1)S(1)}, bf16[8,64,64]{2,1,0:T(8,128)(2,1)S(1)}, u32[]{:S(2)}, u32[]{:S(2)}) collective-permute-start(bf16[8,64,64]{2,1,0:T(8,128)(2,1)S(1)} %fusion.267), channel_id=1, source_target_pairs={{0,4},{4,8},{8,12},{12,16},{16,20},{20,24},{24,28},{1,5},{5,9},{9,... | collective-permute-start | bytes 196616 | tf_op jit(solution)/shard_map/while/body/eval_jaxpr/ppermute | solution.py:15
  552.0 8.9 %collective-permute-start = (bf16[8,64,64]{2,1,0:T(8,128)(2,1)S(1)}, bf16[8,64,64]{2,1,0:T(8,128)(2,1)S(1)}, u32[]{:S(2)}, u32[]{:S(2)}) collective-permute-start(bf16[8,64,64]{2,1,0:T(8,128)(2,1)S(1)} %fusion.267), channel_id=1, source_target_pairs={{0,4},{4,8},{8,12},{12,16},{16,20},{20,24},{24,28},{1,5},{5,9},{9,... | collective-permute-start | bytes 196616 | tf_op jit(solution)/shard_map/while/body/eval_jaxpr/ppermute | solution.py:15
  561.3 7.5 %collective-permute-start = (bf16[8,64,64]{2,1,0:T(8,128)(2,1)S(1)}, bf16[8,64,64]{2,1,0:T(8,128)(2,1)S(1)}, u32[]{:S(2)}, u32[]{:S(2)}) collective-permute-start(bf16[8,64,64]{2,1,0:T(8,128)(2,1)S(1)} %fusion.267), channel_id=1, source_target_pairs={{0,4},{4,8},{8,12},{12,16},{16,20},{20,24},{24,28},{1,5},{5,9},{9,... | collective-permute-start | bytes 196616 | tf_op jit(solution)/shard_map/while/body/eval_jaxpr/ppermute | solution.py:15
  576.0 5.5 copy-start.12
  576.0 6.6 copy-start.15
  582.6 76.6 %copy-start.8 = (bf16[384,512]{1,0:T(8,128)(2,1)S(1)}, bf16[384,512]{1,0:T(8,128)(2,1)}, u32[]{:S(2)}) copy-start(bf16[384,512]{1,0:T(8,128)(2,1)} %param.26) | copy-start | bytes 1179652
  582.6 76.6 %reduce-scatter.2.cloned.1.call-start = ((), (), s32[]{:S(2)}) async-start(), calls=%async_computation.1 | async-start | bytes 1966080 | tf_op jit(solution)/shard_map/reduce_scatter | solution.py:234
  (22 other events, 73.1 us)
Sparse Core Ops, SparseCore 0:
  582.7 74.7 all-reduce.5
Sparse Core Ops, SparseCore 1:
  586.8 32.0 reduce-scatter.1
